TPU v7x, 256 devices: a whole 4x4x8 slice. The times are simulated.
256 devices in a mesh: head: 8 (over y, x_lo), seq: 32 (over z, x_hi, core).
Axes of the slice: x: 4 (x_hi: 2, x_lo: 2; x = x_hi * 2 + x_lo), y: 4, z: 8, core: 2. Of those that a mesh axis runs over, the one named last changes fastest.
Arguments:
- query: bfloat16 [32768, 3072], P(('seq', 'head')), may hold values from -9 to 9
- key: bfloat16 [32768, 3072], P(('seq', 'head')), may hold values from -9 to 9
- value: bfloat16 [32768, 3072], P(('seq', 'head')), may hold values from -6 to 6
- grad_out: bfloat16 [32768, 3072], P(('seq', 'head')), may hold values from -6 to 6
- tile_list: int32 [256, 12], replicated, may hold values from 0 to 255, as said below
- tile_count: int32 [256], replicated, may hold values from 1 to 12, as said below
Outputs:
- attn_out: bfloat16 [32768, 3072], P(('seq', 'head'))
- grad_query: bfloat16 [32768, 3072], P(('seq', 'head'))
- grad_key: bfloat16 [32768, 3072], P(('seq', 'head'))
- grad_value: bfloat16 [32768, 3072], P(('seq', 'head'))
Inputs may be any that keep to these rules, and one draw needn't show every extreme that they name: `tile_list`: tile g sits at frame block g // 8, tile row (g // 2) % 4 and tile column g % 2. Row a lists only tiles at most one step from tile a along each of the three tile axes; its first entry is a itself; its first tile_count[a] entries are distinct; entries from tile_count[a] on are to be ignored. `tile_count`: the number of used entries of each row of tile_list.
All inputs are finite; a program needn't handle non-finite values.
Results may differ from a plain program's by a relative error of at most 0.012.
The roundings to bfloat16 on the way count: a program that leaves them out, or rounds other values in their place, can miss the bound.
Values may be sent and summed in bfloat16 or wider, within the bound.
A program may use at most 128 MiB of HBM per device.

v0:
```python
import jax
import jax.numpy as jnp
from jax import lax
from jax.sharding import PartitionSpec as P

HD = 128
TILE = 128
TILES_DEV = 8
SLAB = 1024


def padded(cells, sides, width):
    for axis, dim in sides:
        count = lax.axis_size(axis)
        ends = count - 1
        head = lax.slice_in_dim(cells, 0, width, axis=dim)
        tail = lax.slice_in_dim(cells, cells.shape[dim] - width, cells.shape[dim], axis=dim)
        cells = jnp.concatenate(
            [
                lax.ppermute(tail, axis, [(i, (i + 1) % count) for i in range(ends)]),
                cells,
                lax.ppermute(head, axis, [((i + 1) % count, i) for i in range(ends)]),
            ],
            axis=dim,
        )
    return cells


def passed_along(block, axis, distance):
    devices = range(lax.axis_size(axis))
    route = [(i - distance, i) for i in devices if i - distance in devices]
    return lax.ppermute(block, axis, route)


def tile_scores(query_tiles, key_tiles, scaling):
    return (
        jnp.einsum("tqhd,tkhd->thqk", query_tiles, key_tiles, preferred_element_type=jnp.float32)
        * scaling
    )


def selector(slots, width, dtype):
    return (slots[:, None] == jnp.arange(width, dtype=jnp.int32)[None, :]).astype(dtype)


def pick_tiles(pool, slots):
    chooser = selector(slots, pool.shape[0], pool.dtype)
    picked = jnp.einsum("tp,pkhd->tkhd", chooser, pool, preferred_element_type=jnp.float32)
    return picked.astype(pool.dtype)


def spread_tiles(values, slots, width):
    chooser = selector(slots, width, jnp.float32)
    return jnp.einsum("tp,tkhd->pkhd", chooser, values, precision=lax.Precision.HIGHEST)


def tile_grads(
    query_tiles, cotangent_tiles, key_tiles, value_tiles, log_total, row_delta, in_use, scaling
):
    score = tile_scores(query_tiles, key_tiles, scaling)
    probability = jnp.where(in_use, jnp.exp(score - log_total[..., None]), 0.0)
    prob_b = probability.astype(jnp.bfloat16)
    grad_prob = jnp.einsum(
        "tqhd,tkhd->thqk", cotangent_tiles, value_tiles, preferred_element_type=jnp.float32
    )
    grad_score = (probability * (grad_prob - row_delta[..., None])).astype(jnp.bfloat16)
    key_grad = jnp.einsum(
        "thqk,tqhd->tkhd", grad_score, query_tiles, preferred_element_type=jnp.float32
    )
    value_grad = jnp.einsum(
        "thqk,tqhd->tkhd", prob_b, cotangent_tiles, preferred_element_type=jnp.float32
    )
    return (grad_score, key_grad, value_grad)


def per_device(query, key, value, grad_out, tile_list, tile_count):
    scaling = HD ** (-0.5)
    slab_index = lax.axis_index("seq")
    query_heads, key_heads, value_heads, cotangent_heads = (
        lax.all_to_all(query, "head", split_axis=1, concat_axis=0, tiled=True),
        lax.all_to_all(key, "head", split_axis=1, concat_axis=0, tiled=True),
        lax.all_to_all(value, "head", split_axis=1, concat_axis=0, tiled=True),
        lax.all_to_all(grad_out, "head", split_axis=1, concat_axis=0, tiled=True),
    )
    columns = query_heads.shape[1]
    heads_dev = columns // HD
    tile_shape = (TILES_DEV, TILE, heads_dev, HD)
    query_tiles = query_heads.reshape(tile_shape)
    key_value = jnp.stack([key_heads, value_heads])
    with_rims = padded(key_value, (("seq", 1),), SLAB)
    kv_pool = with_rims.reshape(2, 3 * TILES_DEV, TILE, heads_dev, HD)
    keys_pool = kv_pool[0]
    values_pool = kv_pool[1]
    pool_width = 3 * TILES_DEV
    own_list = lax.dynamic_slice_in_dim(tile_list, slab_index * TILES_DEV, TILES_DEV, 0)
    own_count = lax.dynamic_slice_in_dim(tile_count, slab_index * TILES_DEV, TILES_DEV, 0)
    pool_slots = (own_list // TILES_DEV - slab_index + 1) * TILES_DEV + own_list % TILES_DEV
    busiest = jnp.max(own_count)

    def norm_pass(slot_index, running):
        running_max, row_total = running
        picked = lax.dynamic_index_in_dim(pool_slots, slot_index, 1, keepdims=False)
        score = tile_scores(query_tiles, pick_tiles(keys_pool, picked), scaling)
        in_use = (slot_index < own_count)[:, None, None]
        new_max = jnp.where(in_use, jnp.maximum(running_max, jnp.max(score, axis=3)), running_max)
        added = jnp.where(in_use, jnp.sum(jnp.exp(score - new_max[..., None]), axis=3), 0.0)
        return (new_max, row_total * jnp.exp(running_max - new_max) + added)

    stat_shape = (TILES_DEV, heads_dev, TILE)
    running_max, row_total = lax.fori_loop(
        0,
        busiest,
        norm_pass,
        (jnp.full(stat_shape, -jnp.inf, jnp.float32), jnp.zeros(stat_shape, jnp.float32)),
    )
    log_total = running_max + jnp.log(row_total)

    def value_pass(slot_index, accum):
        picked = lax.dynamic_index_in_dim(pool_slots, slot_index, 1, keepdims=False)
        score = tile_scores(query_tiles, pick_tiles(keys_pool, picked), scaling)
        in_use = (slot_index < own_count)[:, None, None, None]
        prob_b = jnp.where(in_use, jnp.exp(score - log_total[..., None]), 0.0).astype(jnp.bfloat16)
        return accum + jnp.einsum(
            "thqk,tkhd->tqhd",
            prob_b,
            pick_tiles(values_pool, picked),
            preferred_element_type=jnp.float32,
        )

    attn_tiles = lax.fori_loop(0, busiest, value_pass, jnp.zeros(tile_shape, jnp.float32)).astype(
        jnp.bfloat16
    )
    attn_heads = attn_tiles.reshape(SLAB, columns)
    attn_out = lax.all_to_all(attn_heads, "head", split_axis=0, concat_axis=1, tiled=True)
    cotangent_tiles = cotangent_heads.reshape(tile_shape)
    attn_wide = lax.optimization_barrier(attn_tiles).astype(jnp.float32)
    row_delta = jnp.transpose(
        jnp.sum(cotangent_tiles.astype(jnp.float32) * attn_wide, axis=3), (0, 2, 1)
    )

    def backward_pass(slot_index, carried):
        grad_accum, pool_key, pool_value = carried
        picked = lax.dynamic_index_in_dim(pool_slots, slot_index, 1, keepdims=False)
        key_tiles = pick_tiles(keys_pool, picked)
        in_use = (slot_index < own_count)[:, None, None, None]
        grad_score, key_grad, value_grad = tile_grads(
            query_tiles,
            cotangent_tiles,
            key_tiles,
            pick_tiles(values_pool, picked),
            log_total,
            row_delta,
            in_use,
            scaling,
        )
        grad_accum = grad_accum + jnp.einsum(
            "thqk,tkhd->tqhd", grad_score, key_tiles, preferred_element_type=jnp.float32
        )
        pool_key = pool_key + spread_tiles(key_grad, picked, pool_width)
        pool_value = pool_value + spread_tiles(value_grad, picked, pool_width)
        return (grad_accum, pool_key, pool_value)

    empty_pool = jnp.zeros((pool_width,) + tile_shape[1:], jnp.float32)
    grad_accum, pool_key, pool_value = lax.fori_loop(
        0, busiest, backward_pass, (jnp.zeros(tile_shape, jnp.float32), empty_pool, empty_pool)
    )
    own_key = pool_key[TILES_DEV : 2 * TILES_DEV]
    own_value = pool_value[TILES_DEV : 2 * TILES_DEV]
    lower_part = jnp.stack([pool_key[:TILES_DEV], pool_value[:TILES_DEV]]).astype(jnp.bfloat16)
    upper_part = jnp.stack([pool_key[2 * TILES_DEV :], pool_value[2 * TILES_DEV :]]).astype(
        jnp.bfloat16
    )
    from_below = passed_along(upper_part, "seq", 1).astype(jnp.float32)
    from_above = passed_along(lower_part, "seq", -1).astype(jnp.float32)
    grad_key_sum = own_key + from_below[0] + from_above[0]
    grad_value_sum = own_value + from_below[1] + from_above[1]
    query_grad = (scaling * grad_accum).astype(jnp.bfloat16).reshape(SLAB, columns)
    key_grad_out = (scaling * grad_key_sum).astype(jnp.bfloat16).reshape(SLAB, columns)
    value_grad_out = grad_value_sum.astype(jnp.bfloat16).reshape(SLAB, columns)
    grad_query, grad_key, grad_value = (
        lax.all_to_all(query_grad, "head", split_axis=0, concat_axis=1, tiled=True),
        lax.all_to_all(key_grad_out, "head", split_axis=0, concat_axis=1, tiled=True),
        lax.all_to_all(value_grad_out, "head", split_axis=0, concat_axis=1, tiled=True),
    )
    return (attn_out, grad_query, grad_key, grad_value)


def solution(mesh):
    placed = (
        P(("seq", "head"), None),
        P(("seq", "head"), None),
        P(("seq", "head"), None),
        P(("seq", "head"), None),
        P(),
        P(),
    )
    return jax.shard_map(
        per_device,
        mesh=mesh,
        in_specs=placed,
        out_specs=(
            P(("seq", "head"), None),
            P(("seq", "head"), None),
            P(("seq", "head"), None),
            P(("seq", "head"), None),
        ),
        check_vma=False,
    )
```

profile of v0, /device:TPU:1, one launch (start us, length us, event | category | flops | bytes accessed | tf_op | source)
XLA Modules:
  0.0 647.6 jit_solution(8043777818952585101)
XLA Ops:
  3.3 5.9 all-to-all-start
  10.8 10.1 %all-to-all-done = bf16[128,8,384]{2,0,1:T(8,128)(2,1)S(1)} async-done(((bf16[128,8,384]{2,0,1:T(8,128)(2,1)}), bf16[128,8,384]{2,0,1:T(8,128)(2,1)S(1)}, u32[]{:S(2)}, u32[]{:S(2)}) %all-to-all-start) | async-done | bytes 786464 | tf_op jit(solution)/shard_map/all_to_all | solution.py:81
  25.0 10.9 %all-to-all-done.1 = bf16[128,8,384]{2,0,1:T(8,128)(2,1)S(1)} async-done(((bf16[128,8,384]{2,0,1:T(8,128)(2,1)}), bf16[128,8,384]{2,0,1:T(8,128)(2,1)S(1)}, u32[]{:S(2)}, u32[]{:S(2)}) %all-to-all-start.1) | async-done | bytes 786464 | tf_op jit(solution)/shard_map/all_to_all | solution.py:82
  37.5 4.8 collective-permute-start.1
  52.5 39.9 %all-to-all-done.2 = bf16[128,8,384]{0,2,1:T(8,128)(2,1)S(1)} async-done(((bf16[128,8,384]{0,2,1:T(8,128)(2,1)}), bf16[128,8,384]{0,2,1:T(8,128)(2,1)S(1)}, u32[]{:S(2)}, u32[]{:S(2)}) %all-to-all-start.2) | async-done | bytes 786464 | tf_op jit(solution)/shard_map/all_to_all | solution.py:80
  98.3 6.6 %all-to-all-done.4 = bf16[128,8,384]{0,2,1:T(8,128)(2,1)S(1)} async-done(((bf16[128,8,384]{0,2,1:T(8,128)(2,1)}), bf16[128,8,384]{0,2,1:T(8,128)(2,1)S(1)}, u32[]{:S(2)}, u32[]{:S(2)}) %all-to-all-start.4) | async-done | bytes 786464 | tf_op jit(solution)/shard_map/all_to_all | solution.py:83
  115.7 28.3 %while.36 = (s32[]{:T(128)}, f32[8,3,128]{2,1,0:T(4,128)S(1)}, f32[8,3,128]{2,1,0:T(4,128)S(1)}, s32[]{:T(128)}, s32[8]{0:T(128)S(1)}, /*index=5*/s32[8,12]{0,1:...) while((s32[]{:T(128)}, f32[8,3,128]{2,1,0:T(4,128)S(1)}, ...), condition=%wide.region_4.5_spmd, body=%wide.region_1.4_spmd.sunk | while | flops 121516232 | bytes 8024375 | solution.py:110
  147.7 4.7 copy.79
  153.8 96.1 %while.37 = (s32[]{:T(128)}, f32[8,128,3,128]{1,3,2,0:T(8,128)}, s32[]{:T(128)}, s32[8,12]{0,1:T(8,128)S(1)}, bf16[24,128,3,128]{3,0,2,1:T(8,128)(2,1)}, /*index...) while((s32[]{:T(128)}, f32[8,128,3,128]{1,3,2,0:T(8,128)}, ...), condition=%wide.region_6.7_spmd, body=%wide.region_5.6_spmd.sunk | while | flops 241828240 | bytes 21246324 | solution.py:130
  260.2 285.3 %while.38 = (s32[]{:T(128)}, f32[8,128,3,128]{1,3,2,0:T(8,128)}, f32[24,128,3,128]{3,0,2,1:T(8,128)}, f32[24,128,3,128]{3,0,2,1:T(8,128)}, s32[]{:T(128)}, /*ind...) while((s32[]{:T(128)}, f32[8,128,3,128]{1,3,2,0:T(8,128)}, ...), condition=%wide.region_9.10_spmd, body=%wide.region_8.9_spmd.sunk | while | flops 773849856 | bytes 136864496 | solution.py:164
  273.3 4.3 convolution_add_fusion.4
  277.6 4.3 convolution_add_fusion.5
  297.0 4.3 convolution_add_fusion.4
  301.3 4.3 convolution_add_fusion.5
  320.6 4.3 convolution_add_fusion.4
  325.0 4.3 convolution_add_fusion.5
  344.3 4.3 convolution_add_fusion.4
  348.7 4.3 convolution_add_fusion.5
  368.0 4.3 convolution_add_fusion.4
  372.4 4.3 convolution_add_fusion.5
  439.1 4.3 convolution_add_fusion.4
  462.8 4.3 convolution_add_fusion.4
  467.2 4.3 convolution_add_fusion.5
  486.5 4.3 convolution_add_fusion.4
  490.9 4.3 convolution_add_fusion.5
  514.6 4.3 convolution_add_fusion.5
  538.3 4.3 convolution_add_fusion.5
  545.5 6.1 copy.91
  554.4 6.1 copy.89
  568.1 5.3 collective-permute-start.2
  578.3 25.4 %all-to-all-done.3 = bf16[8,128,384]{1,2,0:T(8,128)(2,1)S(1)} async-done(((bf16[8,128,384]{1,2,0:T(8,128)(2,1)}), bf16[8,128,384]{1,2,0:T(8,128)(2,1)S(1)}, u32[]{:S(2)}, u32[]{:S(2)}) %all-to-all-start.3) | async-done | bytes 786464 | tf_op jit(solution)/shard_map/all_to_all | solution.py:134
  624.1 9.5 %all-to-all-done.6 = bf16[8,128,384]{2,1,0:T(8,128)(2,1)S(1)} async-done(((bf16[8,128,384]{2,1,0:T(8,128)(2,1)}), bf16[8,128,384]{2,1,0:T(8,128)(2,1)S(1)}, u32[]{:S(2)}, u32[]{:S(2)}) %all-to-all-start.6) | async-done | bytes 786464 | tf_op jit(solution)/shard_map/all_to_all | solution.py:182
  (680 shorter events, 412.8 us)
Async XLA Ops:
  2.1 7.1 %copy-start.15 = (bf16[128,3072]{1,0:T(8,128)(2,1)S(1)}, bf16[128,3072]{1,0:T(8,128)(2,1)}, u32[]{:S(2)}) copy-start(bf16[128,3072]{1,0:T(8,128)(2,1)} %param.14) | copy-start | bytes 2359300
  3.3 17.6 %all-to-all-start = ((bf16[128,8,384]{2,0,1:T(8,128)(2,1)}), bf16[128,8,384]{2,0,1:T(8,128)(2,1)S(1)}, u32[]{:S(2)}, u32[]{:S(2)}) async-start(bf16[128,8,384]{2,0,1:T(8,128)(2,1)} %copy.71), calls=%async_computation | async-start | bytes 1572864 | tf_op jit(solution)/shard_map/all_to_all | solution.py:81
  20.9 15.0 %all-to-all-start.1 = ((bf16[128,8,384]{2,0,1:T(8,128)(2,1)}), bf16[128,8,384]{2,0,1:T(8,128)(2,1)S(1)}, u32[]{:S(2)}, u32[]{:S(2)}) async-start(bf16[128,8,384]{2,0,1:T(8,128)(2,1)} %copy.73), calls=%async_computation.1 | async-start | bytes 1572864 | tf_op jit(solution)/shard_map/all_to_all | solution.py:82
  36.2 10.4 %copy-start.16 = (bf16[128,3072]{1,0:T(8,128)(2,1)S(1)}, bf16[128,3072]{1,0:T(8,128)(2,1)}, u32[]{:S(2)}) copy-start(bf16[128,3072]{1,0:T(8,128)(2,1)} %param.12) | copy-start | bytes 2359300
  37.5 13.8 %copy-start.17 = (bf16[128,3072]{1,0:T(8,128)(2,1)S(1)}, bf16[128,3072]{1,0:T(8,128)(2,1)}, u32[]{:S(2)}) copy-start(bf16[128,3072]{1,0:T(8,128)(2,1)} %param.15) | copy-start | bytes 2359300
  37.5 68.6 %collective-permute-start.1 = (bf16[2,1024,384]{1,2,0:T(8,128)(2,1)}, bf16[2,1024,384]{1,2,0:T(8,128)(2,1)}, u32[]{:S(2)}, u32[]{:S(2)}) collective-permute-start(bf16[2,1024,384]{1,2,0:T(8,128)(2,1)} %pad_maximum_fusion.1), channel_id=1, source_target_pairs={{1,0},{2,1},{3,2},{4,3},{5,4},{6,5},{7,6},{8,7},{9,8},{10,9},{11,1... | collective-permute-start | bytes 4718600 | tf_op jit(solution)/shard_map/ppermute | solution.py:22
  42.3 63.8 %collective-permute-start = (bf16[2,1024,384]{1,2,0:T(8,128)(2,1)}, bf16[2,1024,384]{1,2,0:T(8,128)(2,1)}, u32[]{:S(2)}, u32[]{:S(2)}) collective-permute-start(bf16[2,1024,384]{1,2,0:T(8,128)(2,1)} %pad_maximum_fusion.1), channel_id=1, source_target_pairs={{0,1},{1,2},{2,3},{3,4},{4,5},{5,6},{6,7},{7,8},{8,9},{9,10},{10,1... | collective-permute-start | bytes 4718600 | tf_op jit(solution)/shard_map/ppermute | solution.py:20
  47.8 44.7 %all-to-all-start.2 = ((bf16[128,8,384]{0,2,1:T(8,128)(2,1)}), bf16[128,8,384]{0,2,1:T(8,128)(2,1)S(1)}, u32[]{:S(2)}, u32[]{:S(2)}) async-start(bf16[128,8,384]{0,2,1:T(8,128)(2,1)} %bitcast.22), calls=%async_computation.2 | async-start | bytes 1572864 | tf_op jit(solution)/shard_map/all_to_all | solution.py:80
  51.3 44.7 %copy-start.19 = (s32[256]{0:T(256)S(1)}, s32[256]{0:T(256)}, u32[]{:S(2)}) copy-start(s32[256]{0:T(256)} %param.17) | copy-start | bytes 3076
  51.3 45.4 %copy-start.18 = (s32[256,12]{0,1:T(8,128)S(1)}, s32[256,12]{0,1:T(8,128)}, u32[]{:S(2)}) copy-start(s32[256,12]{0,1:T(8,128)} %param.16) | copy-start | bytes 36868
  92.5 12.5 %all-to-all-start.4 = ((bf16[128,8,384]{0,2,1:T(8,128)(2,1)}), bf16[128,8,384]{0,2,1:T(8,128)(2,1)S(1)}, u32[]{:S(2)}, u32[]{:S(2)}) async-start(bf16[128,8,384]{0,2,1:T(8,128)(2,1)} %bitcast.208), calls=%async_computation.4 | async-start | bytes 1572864 | tf_op jit(solution)/shard_map/all_to_all | solution.py:83
  272.1 5.5 slice-start
  295.8 5.5 slice-start
  319.5 5.5 slice-start
  343.2 5.5 slice-start
  366.9 5.5 slice-start
  390.6 5.5 slice-start
  414.3 5.5 slice-start
  438.0 5.5 slice-start
  461.6 5.5 slice-start
  485.3 5.5 slice-start
  509.0 5.5 slice-start
  532.7 5.5 slice-start
  564.8 43.1 %collective-permute-start.3 = (bf16[2,8,128,3,128]{2,4,3,1,0:T(8,128)(2,1)}, bf16[2,8,128,3,128]{2,4,3,1,0:T(8,128)(2,1)}, u32[]{:S(2)}, u32[]{:S(2)}) collective-permute-start(bf16[2,8,128,3,128]{2,4,3,1,0:T(8,128)(2,1)} %pad_maximum_fusion.3), channel_id=1, source_target_pairs={{1,0},{2,1},{3,2},{4,3},{5,4},{6,5},{7,6},{8,7},{9,8},{10,9},{11,1... | collective-permute-start | bytes 4718600 | tf_op jit(solution)/shard_map/ppermute | solution.py:32
  568.1 8.8 %copy-start.8 = (f32[8,128,3,128]{1,3,2,0:T(8,128)S(1)}, f32[8,128,3,128]{1,3,2,0:T(8,128)}, u32[]{:S(2)}) copy-start(f32[8,128,3,128]{1,3,2,0:T(8,128)} %get-tuple-element.169) | copy-start | bytes 4718596
  568.1 41.7 %collective-permute-start.2 = (bf16[2,8,128,3,128]{2,4,3,1,0:T(8,128)(2,1)}, bf16[2,8,128,3,128]{2,4,3,1,0:T(8,128)(2,1)}, u32[]{:S(2)}, u32[]{:S(2)}) collective-permute-start(bf16[2,8,128,3,128]{2,4,3,1,0:T(8,128)(2,1)} %pad_maximum_fusion.2), channel_id=1, source_target_pairs={{0,1},{1,2},{2,3},{3,4},{4,5},{5,6},{6,7},{7,8},{8,9},{9,10},{10,1... | collective-permute-start | bytes 4718600 | tf_op jit(solution)/shard_map/ppermute | solution.py:32
  573.3 30.3 %all-to-all-start.3 = ((bf16[8,128,384]{1,2,0:T(8,128)(2,1)}), bf16[8,128,384]{1,2,0:T(8,128)(2,1)S(1)}, u32[]{:S(2)}, u32[]{:S(2)}) async-start(bf16[8,128,384]{1,2,0:T(8,128)(2,1)} %bitcast.26), calls=%async_computation.3 | async-start | bytes 1572864 | tf_op jit(solution)/shard_map/all_to_all | solution.py:134
  603.7 15.3 %all-to-all-start.5 = ((bf16[8,128,384]{2,1,0:T(8,128)(2,1)}), bf16[8,128,384]{2,1,0:T(8,128)(2,1)}, u32[]{:S(2)}, u32[]{:S(2)}) async-start(bf16[8,128,384]{2,1,0:T(8,128)(2,1)} %copy.87), calls=%async_computation.5 | async-start | bytes 1572864 | tf_op jit(solution)/shard_map/all_to_all | solution.py:181
  615.5 7.4 %copy-start.14 = (bf16[8,128,3,128]{1,3,2,0:T(8,128)(2,1)S(1)}, bf16[8,128,3,128]{1,3,2,0:T(8,128)(2,1)}, u32[]{:S(2)}) copy-start(bf16[8,128,3,128]{1,3,2,0:T(8,128)(2,1)} %get-tuple-element.355) | copy-start | bytes 2359300
  618.9 14.6 %all-to-all-start.6 = ((bf16[8,128,384]{2,1,0:T(8,128)(2,1)}), bf16[8,128,384]{2,1,0:T(8,128)(2,1)S(1)}, u32[]{:S(2)}, u32[]{:S(2)}) async-start(bf16[8,128,384]{2,1,0:T(8,128)(2,1)} %copy.92), calls=%async_computation.6 | async-start | bytes 1572864 | tf_op jit(solution)/shard_map/all_to_all | solution.py:182
  622.9 14.2 %copy-start.12 = (bf16[8,128,384]{1,2,0:T(8,128)(2,1)S(1)}, bf16[8,128,384]{1,2,0:T(8,128)(2,1)}, u32[]{:S(2)}) copy-start(bf16[8,128,384]{1,2,0:T(8,128)(2,1)} %copy-done.11) | copy-start | bytes 2359300
  633.6 12.5 %all-to-all-start.7 = ((bf16[8,128,384]{2,1,0:T(8,128)(2,1)}), bf16[8,128,384]{2,1,0:T(8,128)(2,1)S(1)}, u32[]{:S(2)}, u32[]{:S(2)}) async-start(bf16[8,128,384]{2,1,0:T(8,128)(2,1)} %copy.95), calls=%async_computation.7 | async-start | bytes 1572864 | tf_op jit(solution)/shard_map/all_to_all | solution.py:183
  (136 other events, 312.0 us)
where the time goes:
time: 651 us; the launch traced here: 648 us
  matrix products  301 us (46%)
  local copies, waits for them, and re-layouts  135 us (21%)
  waiting for transfers between devices  107 us (16%)
  starting transfers between devices  48.4 us (7%)
  other arithmetic  30 us (5%)
  loops' own time  25.1 us (4%)
    dot_general x24, matrix products, spread_tiles(): jnp.einsum('tp,tkhd->pkhd', chooser, values, precision=lax.Precision.HIGH...  103 us
    dot_general x60, matrix products, pick_tiles(): jnp.einsum('tp,pkhd->tkhd', chooser, pool, preferred_element_type=jnp.flo...  94.9 us
    while x300, local copies, waits for them, and re-layouts  48.6 us
    dot_general x12, matrix products, value_pass(): jnp.einsum('thqk,tkhd->tqhd', prob_b, pick_tiles(values_pool, picked), pr...  48 us
    all_to_all x1, waiting for transfers between devices, per_device(): lax.all_to_all(query, 'head', split_axis=1, concat_axis=0, tiled=True)  39.9 us
    dot_general x24, matrix products, tile_scores(): jnp.einsum('tqhd,tkhd->thqk', query_tiles, key_tiles, preferred_element_t...  31.6 us
    convert_element_type x12, local copies, waits for them, and re-layouts, pick_tiles(): return picked.astype(pool.dtype)  28.9 us
    all_to_all x1, waiting for transfers between devices, per_device(): lax.all_to_all(attn_heads, 'head', split_axis=0, concat_axis=1, tiled=True)  25.4 us
  transfers between devices with their start and end apart: 12, of which 8 were waited for; matrix products, arithmetic and copies ran while one was open for 4% of the time, Pallas kernels for 0%

commit v1 on v0

--- a/solution.py
+++ b/solution.py
@@ -74,10 +74,16 @@
 
 
 def per_device(query, key, value, grad_out, tile_list, tile_count):
+
+    def _post_islands(local_block):
+        part_next = lax.axis_size("head")
+        right_arr = jnp.stack(jnp.split(local_block, part_next, 1))
+        return jnp.concatenate(lax.all_to_all(right_arr, "head", 0, 0), 0)
+
     scaling = HD ** (-0.5)
     slab_index = lax.axis_index("seq")
     query_heads, key_heads, value_heads, cotangent_heads = (
-        lax.all_to_all(query, "head", split_axis=1, concat_axis=0, tiled=True),
+        _post_islands(query),
         lax.all_to_all(key, "head", split_axis=1, concat_axis=0, tiled=True),
         lax.all_to_all(value, "head", split_axis=1, concat_axis=0, tiled=True),
         lax.all_to_all(grad_out, "head", split_axis=1, concat_axis=0, tiled=True),

time: 651 us -> 643 us (0.988)
  waiting for transfers between devices: 107 us -> 93.6 us
    all_to_all x1, waiting for transfers between devices: 6.62 us -> 0.01 us  [per_device(): lax.all_to_all(grad_out, 'head', split_axis=1, concat_axis=0, tiled=True)]
    unnamed x35 -> x41, local copies, waits for them, and re-layouts: 16.4 us -> 22.6 us
  transfers between devices with their start and end apart: 12 -> 12, of which waited for: 8 -> 7; matrix products, arithmetic and copies ran while one was open for 4% -> 5% of each run, Pallas kernels for 0% -> 0%
where the time goes in v1:
time: 643 us; the launch traced here: 640 us
  matrix products  301 us (47%)
  local copies, waits for them, and re-layouts  139 us (22%)
  waiting for transfers between devices  93.6 us (15%)
  starting transfers between devices  49.4 us (8%)
  other arithmetic  29.5 us (5%)
  loops' own time  25.9 us (4%)
    dot_general x24, matrix products, spread_tiles(): jnp.einsum('tp,tkhd->pkhd', chooser, values, precision=lax.Precision.HIGH...  103 us
    dot_general x60, matrix products, pick_tiles(): jnp.einsum('tp,pkhd->tkhd', chooser, pool, preferred_element_type=jnp.flo...  94.8 us
    while x300, local copies, waits for them, and re-layouts  48.6 us
    dot_general x12, matrix products, value_pass(): jnp.einsum('thqk,tkhd->tqhd', prob_b, pick_tiles(values_pool, picked), pr...  47.9 us
    all_to_all x1, waiting for transfers between devices, _post_islands(): return jnp.concatenate(lax.all_to_all(right_arr, 'head', 0, 0), 0)  34.2 us
    dot_general x24, matrix products, tile_scores(): jnp.einsum('tqhd,tkhd->thqk', query_tiles, key_tiles, preferred_element_t...  31.6 us
    convert_element_type x12, local copies, waits for them, and re-layouts, pick_tiles(): return picked.astype(pool.dtype)  28.9 us
    all_to_all x1, waiting for transfers between devices, per_device(): lax.all_to_all(attn_heads, 'head', split_axis=0, concat_axis=1, tiled=True)  25.3 us
  transfers between devices with their start and end apart: 12, of which 7 were waited for; matrix products, arithmetic and copies ran while one was open for 5% of the time, Pallas kernels for 0%

profile of v1, /device:TPU:1, one launch (start us, length us, event | category | flops | bytes accessed | tf_op | source)
XLA Modules:
  0.0 639.6 jit_solution(202515376748436058)
XLA Ops:
  3.3 5.9 all-to-all-start
  11.7 9.2 %all-to-all-done = bf16[128,8,384]{2,0,1:T(8,128)(2,1)S(1)} async-done(((bf16[128,8,384]{2,0,1:T(8,128)(2,1)}), bf16[128,8,384]{2,0,1:T(8,128)(2,1)S(1)}, u32[]{:S(2)}, u32[]{:S(2)}) %all-to-all-start) | async-done | bytes 786464 | tf_op jit(solution)/shard_map/all_to_all | solution.py:87
  31.2 4.7 all-to-all-done.1
  41.1 4.8 collective-permute-start.1
  53.1 4.7 all-to-all-start.2
  60.5 34.2 %all-to-all-done.2 = bf16[8,128,384]{1,2,0:T(8,128)(2,1)S(1)} async-done(((bf16[8,128,384]{1,2,0:T(8,128)(2,1)}), bf16[8,128,384]{1,2,0:T(8,128)(2,1)S(1)}, u32[]{:S(2)}, u32[]{:S(2)}) %all-to-all-start.2) | async-done | bytes 786464 | tf_op jit(solution)/shard_map/all_to_all | solution.py:81
  104.7 28.6 %while.36 = (s32[]{:T(128)}, f32[8,3,128]{2,1,0:T(4,128)S(1)}, f32[8,3,128]{2,1,0:T(4,128)S(1)}, s32[]{:T(128)}, s32[8]{0:T(128)S(1)}, /*index=5*/s32[8,12]{0,1:...) while((s32[]{:T(128)}, f32[8,3,128]{2,1,0:T(4,128)S(1)}, ...), condition=%wide.region_4.5_spmd, body=%wide.region_1.4_spmd.sunk | while | flops 121516232 | bytes 8024375 | solution.py:116
  137.0 4.7 copy.100
  143.0 96.4 %while.37 = (s32[]{:T(128)}, f32[8,128,3,128]{1,3,2,0:T(8,128)}, s32[]{:T(128)}, s32[8,12]{0,1:T(8,128)S(1)}, bf16[24,128,3,128]{3,0,2,1:T(8,128)(2,1)}, /*index...) while((s32[]{:T(128)}, f32[8,128,3,128]{1,3,2,0:T(8,128)}, ...), condition=%wide.region_6.7_spmd, body=%wide.region_5.6_spmd.sunk | while | flops 241828240 | bytes 21246324 | solution.py:136
  249.7 285.5 %while.38 = (s32[]{:T(128)}, f32[8,128,3,128]{1,3,2,0:T(8,128)}, f32[24,128,3,128]{3,0,2,1:T(8,128)}, f32[24,128,3,128]{3,0,2,1:T(8,128)}, s32[]{:T(128)}, /*ind...) while((s32[]{:T(128)}, f32[8,128,3,128]{1,3,2,0:T(8,128)}, ...), condition=%wide.region_9.10_spmd, body=%wide.region_8.9_spmd.sunk | while | flops 773849856 | bytes 136864496 | solution.py:170
  262.7 4.3 convolution_add_fusion.4
  286.4 4.3 convolution_add_fusion.4
  290.8 4.3 convolution_add_fusion.5
  333.9 4.3 convolution_add_fusion.4
  338.2 4.3 convolution_add_fusion.5
  357.6 4.3 convolution_add_fusion.4
  361.9 4.3 convolution_add_fusion.5
  381.3 4.3 convolution_add_fusion.4
  385.6 4.3 convolution_add_fusion.5
  405.0 4.3 convolution_add_fusion.4
  409.4 4.3 convolution_add_fusion.5
  452.4 4.3 convolution_add_fusion.4
  456.8 4.3 convolution_add_fusion.5
  480.5 4.3 convolution_add_fusion.5
  535.2 6.0 copy.112
  544.0 6.1 copy.110
  557.7 5.3 collective-permute-start.2
  568.0 25.3 %all-to-all-done.3 = bf16[8,128,384]{1,2,0:T(8,128)(2,1)S(1)} async-done(((bf16[8,128,384]{1,2,0:T(8,128)(2,1)}), bf16[8,128,384]{1,2,0:T(8,128)(2,1)S(1)}, u32[]{:S(2)}, u32[]{:S(2)}) %all-to-all-start.3) | async-done | bytes 786464 | tf_op jit(solution)/shard_map/all_to_all | solution.py:140
  593.3 4.4 all-to-all-start.5
  605.3 5.1 all-to-all-done.5
  615.1 10.3 %all-to-all-done.6 = bf16[8,128,384]{2,1,0:T(8,128)(2,1)S(1)} async-done(((bf16[8,128,384]{2,1,0:T(8,128)(2,1)}), bf16[8,128,384]{2,1,0:T(8,128)(2,1)S(1)}, u32[]{:S(2)}, u32[]{:S(2)}) %all-to-all-start.6) | async-done | bytes 786464 | tf_op jit(solution)/shard_map/all_to_all | solution.py:188
  633.3 4.7 all-to-all-done.7
  (688 shorter events, 416.8 us)
Async XLA Ops:
  2.1 7.1 %copy-start.12 = (bf16[128,3072]{1,0:T(8,128)(2,1)S(1)}, bf16[128,3072]{1,0:T(8,128)(2,1)}, u32[]{:S(2)}) copy-start(bf16[128,3072]{1,0:T(8,128)(2,1)} %param.14) | copy-start | bytes 2359300
  3.3 17.6 %all-to-all-start = ((bf16[128,8,384]{2,0,1:T(8,128)(2,1)}), bf16[128,8,384]{2,0,1:T(8,128)(2,1)S(1)}, u32[]{:S(2)}, u32[]{:S(2)}) async-start(bf16[128,8,384]{2,0,1:T(8,128)(2,1)} %copy.85), calls=%async_computation | async-start | bytes 1572864 | tf_op jit(solution)/shard_map/all_to_all | solution.py:87
  10.8 13.9 %copy-start.14 = (bf16[128,3072]{1,0:T(8,128)(2,1)S(1)}, bf16[128,3072]{1,0:T(8,128)(2,1)}, u32[]{:S(2)}) copy-start(bf16[128,3072]{1,0:T(8,128)(2,1)} %param.15) | copy-start | bytes 2359300
  20.9 15.0 %all-to-all-start.1 = ((bf16[128,8,384]{2,0,1:T(8,128)(2,1)}), bf16[128,8,384]{2,0,1:T(8,128)(2,1)S(1)}, u32[]{:S(2)}, u32[]{:S(2)}) async-start(bf16[128,8,384]{2,0,1:T(8,128)(2,1)} %copy.87), calls=%async_computation.1 | async-start | bytes 1572864 | tf_op jit(solution)/shard_map/all_to_all | solution.py:88
  35.9 17.2 %all-to-all-start.4 = ((bf16[128,8,384]{0,2,1:T(8,128)(2,1)}), bf16[128,8,384]{0,2,1:T(8,128)(2,1)S(1)}, u32[]{:S(2)}, u32[]{:S(2)}) async-start(bf16[128,8,384]{0,2,1:T(8,128)(2,1)} %bitcast.34), calls=%async_computation.4 | async-start | bytes 1572864 | tf_op jit(solution)/shard_map/all_to_all | solution.py:89
  41.1 18.2 %copy-start.15 = (s32[256,12]{0,1:T(8,128)S(1)}, s32[256,12]{0,1:T(8,128)}, u32[]{:S(2)}) copy-start(s32[256,12]{0,1:T(8,128)} %param.16) | copy-start | bytes 36868
  41.1 54.1 %collective-permute-start.1 = (bf16[2,1024,384]{1,2,0:T(8,128)(2,1)}, bf16[2,1024,384]{1,2,0:T(8,128)(2,1)}, u32[]{:S(2)}, u32[]{:S(2)}) collective-permute-start(bf16[2,1024,384]{1,2,0:T(8,128)(2,1)} %pad_maximum_fusion.1), channel_id=1, source_target_pairs={{1,0},{2,1},{3,2},{4,3},{5,4},{6,5},{7,6},{8,7},{9,8},{10,9},{11,1... | collective-permute-start | bytes 4718600 | tf_op jit(solution)/shard_map/ppermute | solution.py:22
  45.9 49.3 %collective-permute-start = (bf16[2,1024,384]{1,2,0:T(8,128)(2,1)}, bf16[2,1024,384]{1,2,0:T(8,128)(2,1)}, u32[]{:S(2)}, u32[]{:S(2)}) collective-permute-start(bf16[2,1024,384]{1,2,0:T(8,128)(2,1)} %pad_maximum_fusion.1), channel_id=1, source_target_pairs={{0,1},{1,2},{2,3},{3,4},{4,5},{5,6},{6,7},{7,8},{8,9},{9,10},{10,1... | collective-permute-start | bytes 4718600 | tf_op jit(solution)/shard_map/ppermute | solution.py:20
  53.1 7.4 %copy-start.9 = (bf16[128,8,384]{0,2,1:T(8,128)(2,1)}, bf16[128,8,384]{0,2,1:T(8,128)(2,1)S(1)}, u32[]{:S(2)}) copy-start(bf16[128,8,384]{0,2,1:T(8,128)(2,1)S(1)} %all-to-all-done.4) | copy-start | bytes 2359300
  53.1 41.6 %all-to-all-start.2 = ((bf16[8,128,384]{1,2,0:T(8,128)(2,1)}), bf16[8,128,384]{1,2,0:T(8,128)(2,1)S(1)}, u32[]{:S(2)}, u32[]{:S(2)}) async-start(bf16[8,128,384]{1,2,0:T(8,128)(2,1)} %bitcast_dynamic-update-slice_fusion), calls=%async_computation.2 | async-start | bytes 1572864 | tf_op jit(solution)/shard_map/all_to_all | solution.py:81
  261.5 5.5 slice-start
  262.7 4.3 slice-start.1
  285.3 5.5 slice-start
  286.4 4.3 slice-start.1
  309.0 5.5 slice-start
  332.7 5.5 slice-start
  333.9 4.3 slice-start.1
  356.4 5.5 slice-start
  380.1 5.5 slice-start
  403.8 5.5 slice-start
  427.5 5.5 slice-start
  451.3 5.5 slice-start
  475.0 5.5 slice-start
  498.7 5.5 slice-start
  522.4 5.5 slice-start
  554.5 43.2 %collective-permute-start.3 = (bf16[2,8,128,3,128]{2,4,3,1,0:T(8,128)(2,1)}, bf16[2,8,128,3,128]{2,4,3,1,0:T(8,128)(2,1)}, u32[]{:S(2)}, u32[]{:S(2)}) collective-permute-start(bf16[2,8,128,3,128]{2,4,3,1,0:T(8,128)(2,1)} %pad_maximum_fusion.3), channel_id=1, source_target_pairs={{1,0},{2,1},{3,2},{4,3},{5,4},{6,5},{7,6},{8,7},{9,8},{10,9},{11,1... | collective-permute-start | bytes 4718600 | tf_op jit(solution)/shard_map/ppermute | solution.py:32
  557.7 8.8 %copy-start.8 = (f32[8,128,3,128]{1,3,2,0:T(8,128)S(1)}, f32[8,128,3,128]{1,3,2,0:T(8,128)}, u32[]{:S(2)}) copy-start(f32[8,128,3,128]{1,3,2,0:T(8,128)} %get-tuple-element.169) | copy-start | bytes 4718596
  557.7 41.8 %collective-permute-start.2 = (bf16[2,8,128,3,128]{2,4,3,1,0:T(8,128)(2,1)}, bf16[2,8,128,3,128]{2,4,3,1,0:T(8,128)(2,1)}, u32[]{:S(2)}, u32[]{:S(2)}) collective-permute-start(bf16[2,8,128,3,128]{2,4,3,1,0:T(8,128)(2,1)} %pad_maximum_fusion.2), channel_id=1, source_target_pairs={{0,1},{1,2},{2,3},{3,4},{4,5},{5,6},{6,7},{7,8},{8,9},{9,10},{10,1... | collective-permute-start | bytes 4718600 | tf_op jit(solution)/shard_map/ppermute | solution.py:32
  563.0 30.3 %all-to-all-start.3 = ((bf16[8,128,384]{1,2,0:T(8,128)(2,1)}), bf16[8,128,384]{1,2,0:T(8,128)(2,1)S(1)}, u32[]{:S(2)}, u32[]{:S(2)}) async-start(bf16[8,128,384]{1,2,0:T(8,128)(2,1)} %bitcast.31), calls=%async_computation.3 | async-start | bytes 1572864 | tf_op jit(solution)/shard_map/all_to_all | solution.py:140
  593.3 17.1 %all-to-all-start.5 = ((bf16[8,128,384]{2,1,0:T(8,128)(2,1)}), bf16[8,128,384]{2,1,0:T(8,128)(2,1)S(1)}, u32[]{:S(2)}, u32[]{:S(2)}) async-start(bf16[8,128,384]{2,1,0:T(8,128)(2,1)} %copy.108), calls=%async_computation.5 | async-start | bytes 1572864 | tf_op jit(solution)/shard_map/all_to_all | solution.py:187
  610.4 15.0 %all-to-all-start.6 = ((bf16[8,128,384]{2,1,0:T(8,128)(2,1)}), bf16[8,128,384]{2,1,0:T(8,128)(2,1)S(1)}, u32[]{:S(2)}, u32[]{:S(2)}) async-start(bf16[8,128,384]{2,1,0:T(8,128)(2,1)} %copy.113), calls=%async_computation.6 | async-start | bytes 1572864 | tf_op jit(solution)/shard_map/all_to_all | solution.py:188
  625.4 12.6 %all-to-all-start.7 = ((bf16[8,128,384]{2,1,0:T(8,128)(2,1)}), bf16[8,128,384]{2,1,0:T(8,128)(2,1)S(1)}, u32[]{:S(2)}, u32[]{:S(2)}) async-start(bf16[8,128,384]{2,1,0:T(8,128)(2,1)} %copy.116), calls=%async_computation.7 | async-start | bytes 1572864 | tf_op jit(solution)/shard_map/all_to_all | solution.py:189
  (132 other events, 291.4 us)
